TPU v7x, 128 devices: a whole 4x4x4 slice. The times are simulated.
128 devices in a mesh: tm: 8 (over x, z_hi), pts: 16 (over z_lo, y, core).
Axes of the slice: x: 4, y: 4, z: 4 (z_hi: 2, z_lo: 2; z = z_hi * 2 + z_lo), core: 2. Of those that a mesh axis runs over, the one named last changes fastest.
Arguments:
- psi_rows: bfloat16 [512, 6144], replicated, may hold values from -1.1953125 to 1.1953125
- psi_cols: bfloat16 [6144, 16384], P(None, 'pts'), may hold values from -1.1953125 to 1.1953125
- psi_slab: bfloat16 [1024, 1024], replicated, may hold values from -1.1953125 to 1.1953125
- occ_depth: float32 [1024], replicated, may hold values from 0.05 to 2
- virt_height: float32 [5120], replicated, may hold values from 0.05 to 2
- coulomb: bfloat16 [16384, 1024], P('pts'), may hold values from -0.046875 to 0.046875
Outputs:
- sigma: float32 [512, 16, 1024], P('pts', 'tm')
All inputs are finite; a program needn't handle non-finite values.
Results may differ from a plain program's by a relative error of at most 0.0065.
Values may be sent and summed in bfloat16 or wider, within the bound.
A program may use at most 128 MiB of HBM per device.

v0:
```python
import math

import jax
import jax.numpy as jnp
from jax import lax
from jax.sharding import PartitionSpec as P

NOCC = 1024
TIMES = 16


TIME_SPAN = 8.0
FREQ_SPAN = 8.0


def transform_tables():
    steps = jnp.arange(TIMES, dtype=jnp.float32) + 0.5
    fraction = steps / TIMES
    times_grid = TIME_SPAN * fraction * fraction
    time_weight = TIME_SPAN * 2.0 * fraction / TIMES
    frequency = FREQ_SPAN * fraction * fraction
    freq_weight = FREQ_SPAN * 2.0 * fraction / TIMES
    forward = time_weight[None, :] * jnp.cos(frequency[:, None] * times_grid[None, :])
    backward = (
        2.0 / math.pi * freq_weight[None, :] * jnp.cos(times_grid[:, None] * frequency[None, :])
    )
    return (times_grid, forward, backward)


def per_device(psi_rows, psi_cols, psi_slab, occ_depth, virt_height, coulomb):
    local_times = TIMES // lax.axis_size("tm")
    time_rank = lax.axis_index("tm")
    point_rank = lax.axis_index("pts")
    all_rows = psi_rows.shape[0]
    local_rows = all_rows // lax.axis_size("pts")
    times_grid, forward, backward = transform_tables()
    my_times = lax.dynamic_slice_in_dim(times_grid, time_rank * local_times, local_times)
    occ_rows = psi_rows[:, :NOCC].astype(jnp.float32)
    virt_rows = psi_rows[:, NOCC:].astype(jnp.float32)
    occ_cols = psi_cols[:NOCC]
    virt_cols = psi_cols[NOCC:]
    chi_list = []
    slab_list = []
    for number in range(local_times):
        moment = my_times[number]
        scaled_occ = (occ_rows * jnp.exp(-occ_depth * moment)[None, :]).astype(jnp.bfloat16)
        scaled_virt = (virt_rows * jnp.exp(-virt_height * moment)[None, :]).astype(jnp.bfloat16)
        green_occ = jnp.dot(scaled_occ, occ_cols, preferred_element_type=jnp.float32)
        green_virt = jnp.dot(scaled_virt, virt_cols, preferred_element_type=jnp.float32)
        chi_list.append((green_occ * green_virt).astype(jnp.bfloat16))
        mine = lax.dynamic_slice_in_dim(scaled_occ, point_rank * local_rows, local_rows, 0)
        slab_list.append(jnp.dot(mine, psi_slab, preferred_element_type=jnp.float32))
    chi_time = jnp.stack(chi_list, axis=1)
    piece = lax.all_gather(chi_time, "tm", axis=1, tiled=True)
    weights = lax.dynamic_slice(
        forward, (time_rank * local_times, 0), (local_times, piece.shape[1])
    )
    chi_freq = jnp.einsum(
        "wt,rtp->rwp", weights, piece.astype(jnp.float32), precision=lax.Precision.HIGHEST
    ).astype(jnp.bfloat16)
    screened = lax.psum_scatter(
        jnp.einsum("rwp,pq->rwq", chi_freq, coulomb, preferred_element_type=jnp.float32),
        "pts",
        scatter_dimension=0,
        tiled=True,
    )
    resummed = screened / jnp.sqrt(1.0 + screened * screened)
    piece = lax.all_gather(resummed, "tm", axis=1, tiled=True)
    weights = lax.dynamic_slice(
        backward, (time_rank * local_times, 0), (local_times, piece.shape[1])
    )
    screened_time = jnp.einsum("tw,rwq->rtq", weights, piece, precision=lax.Precision.HIGHEST)
    green_slab = jnp.stack(slab_list, axis=1)
    return green_slab * screened_time


def solution(mesh):
    in_specs = (P(), P(None, "pts"), P(), P(), P(), P("pts", None))
    out_specs = P("pts", "tm", None)
    return jax.shard_map(
        per_device, mesh=mesh, in_specs=in_specs, out_specs=out_specs, check_vma=False
    )
```

profile of v0, /device:TPU:0, one launch (start us, length us, event | category | flops | bytes accessed | tf_op | source)
XLA Modules:
  0.0 386.2 jit_solution(7971587291689427776)
XLA Ops:
  6.6 0.1 dynamic_slice.15
  6.6 0.6 fusion.56
  7.3 2.0 multiply_exponential_fusion.3
  9.2 2.0 multiply_exponential_fusion.1
  11.3 0.0 slice-start
  11.3 1.7 fusion.14
  13.0 0.0 copy-start.2
  13.0 0.0 slice-start.1
  13.0 4.6 %fusion.22 = f32[512,1024]{1,0:T(8,128)} fusion(bf16[512,1024]{1,0:T(8,128)(2,1)S(1)} %get-tuple-element.6, bf16[6144,1024]{1,0:T(8,128)(2,1)} %param.7), kind=kOutput, calls=%fused_computation.27 | convolution fusion | flops 1073741824 | bytes 5242880 | tf_op jit(solution)/shard_map/dot_general | solution.py:48
  17.7 4.3 %fusion.24 = f32[512,1024]{1,0:T(8,128)} fusion(bf16[512,1024]{1,0:T(8,128)(2,1)S(1)} %get-tuple-element.5, bf16[6144,1024]{1,0:T(8,128)(2,1)} %param.7), kind=kOutput, calls=%fused_computation.29 | convolution fusion | flops 1073741824 | bytes 5242880 | tf_op jit(solution)/shard_map/dot_general | solution.py:48
  22.0 0.0 slice-start.4
  22.0 8.7 %fusion.39 = bf16[512,1,1024]{2,0,1:T(8,128)(2,1)S(1)} fusion(f32[512,1024]{1,0:T(8,128)} %fusion.22, bf16[6144,1024]{1,0:T(8,128)(2,1)} %param.7, f32[5120]{0:T(1024)S(1)} %get-tuple-element.8, bf16[512,6144]{1,0:T(8,128)(2,1)S(1)} %bitcast.29), kind=kOutput, calls=%fused_computation.32 | convolution fusion | flops 5377622016 | bytes 18894848 | tf_op jit(solution)/shard_map/dot_general | solution.py:49
  30.7 7.2 %fusion.34 = bf16[512,1,1024]{2,0,1:T(8,128)(2,1)S(1)} fusion(f32[512,1024]{1,0:T(8,128)} %fusion.24, bf16[6144,1024]{1,0:T(8,128)(2,1)S(1)} %bitcast.31, f32[5120]{0:T(1024)S(1)} %get-tuple-element.7, bf16[512,6144]{1,0:T(8,128)(2,1)S(1)} %bitcast.29), kind=kOutput, calls=%fused_computation.31 | convolution fusion | flops 5377622016 | bytes 18894848 | tf_op jit(solution)/shard_map/dot_general | solution.py:49
  37.9 1.5 pad_maximum_fusion
  39.4 0.0 all-gather.3.cloned.1.call-update
  39.4 0.2 reduce-scatter.2.cloned.1.call-start
  39.7 0.1 multiply_cosine_fusion
  39.8 187.8 %all-gather.3.cloned.1.call-done = bf16[512,16,1024]{2,0,1:T(8,128)(2,1)} async-done(((bf16[512,2,1024]{2,0,1:T(8,128)(2,1)}), bf16[512,16,1024]{2,0,1:T(8,128)(2,1)}) %all-gather.3.cloned.1.call-update) | async-done | bytes 16777232 | tf_op jit(solution)/shard_map/all_gather | solution.py:54
  227.5 21.7 %fusion = bf16[512,1024,2]{1,2,0:T(2,128)(2,1)S(1)} fusion(bf16[512,16,1024]{2,0,1:T(8,128)(2,1)} %all-gather.3.cloned.1.call-done, f32[16,16]{1,0:T(8,128)S(1)} %multiply_cosine_fusion, s32[]{:T(128)S(6)} %select_n.4, f32[16]{0:T(128)S(1)} %fusion.55), kind=kOutput, calls=%fused_computation | convolution fusion | flops 201326624 | bytes 18875908 | tf_op jit(solution)/shard_map/wt,rtp->rwp/dot_general | solution.py:58
  249.3 4.3 %fusion.17 = f32[512,2,1024]{2,0,1:T(8,128)} fusion(bf16[512,1024,2]{1,2,0:T(2,128)(2,1)S(1)} %fusion, bf16[1024,1024]{1,0:T(8,128)(2,1)S(1)} %copy-done), kind=kOutput, calls=%fused_computation.20 | convolution fusion | flops 2147483648 | bytes 8388608 | tf_op jit(solution)/shard_map/rwp,pq->rwq/dot_general | solution.py:62
  253.5 0.0 reduce-scatter.2.cloned.1.call-update
  253.5 0.3 all-gather.5.cloned.1.call-start
  253.8 65.1 %reduce-scatter.2.cloned.1.call-done = f32[32,2,1024]{2,0,1:T(8,128)} async-done(((f32[512,2,1024]{2,0,1:T(8,128)}), f32[32,2,1024]{2,0,1:T(8,128)}) %reduce-scatter.2.cloned.1.call-update) | async-done | bytes 262160 | tf_op jit(solution)/shard_map/reduce_scatter | solution.py:61
  318.9 1.7 rsqrt_multiply_fusion
  320.6 0.0 all-gather.5.cloned.1.call-update
  320.7 0.0 copy-start.1
  320.7 2.2 convolution_bitcast_fusion
  322.9 0.5 convolution_bitcast_fusion.1
  323.4 51.4 %all-gather.5.cloned.1.call-done = f32[32,16,1024]{2,0,1:T(8,128)} async-done(((f32[32,2,1024]{2,0,1:T(8,128)}), f32[32,16,1024]{2,0,1:T(8,128)}) %all-gather.5.cloned.1.call-update) | async-done | bytes 2097168 | tf_op jit(solution)/shard_map/all_gather | solution.py:68
  374.8 3.9 fusion.20
  378.6 0.1 maximum_multiply_fusion
  378.7 0.9 copy.12
  (17 shorter events, 0.1 us)
Async XLA Ops:
  6.5 242.7 %copy-start = (bf16[1024,1024]{1,0:T(8,128)(2,1)S(1)}, bf16[1024,1024]{1,0:T(8,128)(2,1)}, u32[]{:S(2)}) copy-start(bf16[1024,1024]{1,0:T(8,128)(2,1)} %param.11) | copy-start | bytes 6291460
  6.5 221.0 %all-gather.3.cloned.1.call-start = ((), (), s32[]{:S(2)}) async-start(), calls=%async_computation.1 | async-start | bytes 18874368 | tf_op jit(solution)/shard_map/all_gather | solution.py:54
  11.3 10.7 %slice-start = ((s8[6291456]{0:T(1024)(128)(4,1)}), s8[4194304]{0:T(1024)(128)(4,1)S(1)}, s32[]{:S(2)}) async-start(s8[6291456]{0:T(1024)(128)(4,1)} %bitcast.28), calls=%async_computation.4 | async-start | bytes 8388608
  13.0 4.6 %copy-start.2 = (bf16[512,1024]{1,0:T(8,128)(2,1)}, bf16[512,1024]{1,0:T(8,128)(2,1)S(1)}, u32[]{:S(2)}) copy-start(bf16[512,1024]{1,0:T(8,128)(2,1)S(1)} %get-tuple-element.6) | copy-start | bytes 3145732
  13.0 8.9 %slice-start.1 = ((s8[6291456]{0:T(1024)(128)(4,1)}), s8[2097152]{0:T(1024)(128)(4,1)S(1)}, s32[]{:S(2)}) async-start(s8[6291456]{0:T(1024)(128)(4,1)} %bitcast.28), calls=%async_computation.5 | async-start | bytes 4194304
  17.7 13.0 %slice-start.2 = ((s8[12582912]{0:T(1024)(128)(4,1)}), s8[4194304]{0:T(1024)(128)(4,1)S(1)}, s32[]{:S(2)}) async-start(s8[12582912]{0:T(1024)(128)(4,1)} %bitcast.30), calls=%async_computation.6 | async-start | bytes 8388608
  21.9 8.7 %slice-start.3 = ((s8[12582912]{0:T(1024)(128)(4,1)}), s8[4194304]{0:T(1024)(128)(4,1)S(1)}, s32[]{:S(2)}) async-start(s8[12582912]{0:T(1024)(128)(4,1)} %bitcast.30), calls=%async_computation.7 | async-start | bytes 8388608
  22.0 8.8 %slice-start.4 = ((s8[12582912]{0:T(1024)(128)(4,1)}), s8[4194304]{0:T(1024)(128)(4,1)S(1)}, s32[]{:S(2)}) async-start(s8[12582912]{0:T(1024)(128)(4,1)} %bitcast.30), calls=%async_computation.8 | async-start | bytes 8388608
  39.4 279.5 %reduce-scatter.2.cloned.1.call-start = ((), (), s32[]{:S(2)}) async-start(), calls=%async_computation.2 | async-start | bytes 4456448 | tf_op jit(solution)/shard_map/reduce_scatter | solution.py:61
  253.5 121.2 %all-gather.5.cloned.1.call-start = ((), (), s32[]{:S(2)}) async-start(), calls=%async_computation.3 | async-start | bytes 2359296 | tf_op jit(solution)/shard_map/all_gather | solution.py:68
  320.7 2.3 copy-start.1
Sparse Core Ops, SparseCore 0:
  39.5 187.9 all-gather.2
  253.7 65.2 reduce-scatter.1
  321.3 53.4 all-gather.4
where the time goes:
time: 386 us
  waiting for transfers between devices  304 us (79%)
  matrix products  57.3 us (15%)
  between operations  13.3 us (3%)
  other arithmetic  9.17 us (2%)
    all_gather x1, waiting for transfers between devices, per_device(): piece = lax.all_gather(chi_time, 'tm', axis=1, tiled=True)  188 us
    reduce_scatter x1, waiting for transfers between devices, per_device(): lax.psum_scatter(jnp.einsum('rwp,pq->rwq', chi_freq, coulomb, preferred_e...  65.1 us
    all_gather x1, waiting for transfers between devices, per_device(): piece = lax.all_gather(resummed, 'tm', axis=1, tiled=True)  51.4 us
    dot_general x1, matrix products, per_device(): jnp.einsum('wt,rtp->rwp', weights, piece.astype(jnp.float32), precision=l...  21.7 us
    dot_general x2, matrix products, per_device(): jnp.dot(scaled_virt, virt_cols, preferred_element_type=jnp.float32)  15.9 us
    dot_general x2, matrix products, per_device(): jnp.dot(scaled_occ, occ_cols, preferred_element_type=jnp.float32)  8.89 us
  transfers between devices with their start and end apart: 3, of which 3 were waited for; matrix products, arithmetic and copies ran while one was open for 1% of the time, Pallas kernels for 0%

commit v1 on v0

v1 whole, which is shorter than its diff:
```python
import math

import jax
import jax.numpy as jnp
from jax import lax
from jax.sharding import PartitionSpec as P

NOCC = 1024
TIMES = 16


TIME_SPAN = 8.0
FREQ_SPAN = 8.0


def transform_tables():
    steps = jnp.arange(TIMES, dtype=jnp.float32) + 0.5
    fraction = steps / TIMES
    times_grid = TIME_SPAN * fraction * fraction
    time_weight = TIME_SPAN * 2.0 * fraction / TIMES
    frequency = FREQ_SPAN * fraction * fraction
    freq_weight = FREQ_SPAN * 2.0 * fraction / TIMES
    forward = time_weight[None, :] * jnp.cos(frequency[:, None] * times_grid[None, :])
    backward = (
        2.0 / math.pi * freq_weight[None, :] * jnp.cos(times_grid[:, None] * frequency[None, :])
    )
    return (times_grid, forward, backward)


def per_device(psi_rows, psi_cols, psi_slab, occ_depth, virt_height, coulomb):
    teams = lax.axis_size("tm")
    owners = lax.axis_size("pts")
    local_times = TIMES // teams
    time_rank = lax.axis_index("tm")
    point_rank = lax.axis_index("pts")
    all_rows, orbitals = psi_rows.shape
    local_rows = all_rows // owners
    share = local_rows // teams
    points = psi_cols.shape[1]
    slab = coulomb.shape[1]
    times_grid, forward, backward = transform_tables()

    dealt = psi_rows.reshape(owners, teams, share, orbitals)
    dealt = lax.dynamic_index_in_dim(dealt, time_rank, 1, keepdims=False)
    dealt = dealt.reshape(owners * share, orbitals).astype(jnp.float32)
    heights = jnp.concatenate([occ_depth, virt_height])
    decay = jnp.exp(-heights[None, :] * times_grid[:, None])
    scaled = (dealt[:, None, :] * decay[None, :, :]).astype(jnp.bfloat16)
    scaled = scaled.reshape(owners * share * TIMES, orbitals)
    green_occ = jnp.dot(scaled[:, :NOCC], psi_cols[:NOCC], preferred_element_type=jnp.float32)
    green_virt = jnp.dot(scaled[:, NOCC:], psi_cols[NOCC:], preferred_element_type=jnp.float32)
    chi_time = (green_occ * green_virt).astype(jnp.bfloat16)
    partial = jnp.dot(chi_time, coulomb, preferred_element_type=jnp.float32)
    summed = lax.psum_scatter(partial, "pts", scatter_dimension=0, tiled=True)
    summed = summed.reshape(share, TIMES, slab)

    screened = jnp.einsum("wt,rtq->rwq", forward, summed, precision=lax.Precision.HIGHEST)
    resummed = screened / jnp.sqrt(1.0 + screened * screened)
    by_time = jnp.einsum("tw,rwq->rtq", backward, resummed, precision=lax.Precision.HIGHEST)
    screened_time = lax.all_to_all(by_time, "tm", split_axis=1, concat_axis=0, tiled=True)

    mine = lax.dynamic_slice_in_dim(psi_rows[:, :NOCC], point_rank * local_rows, local_rows, 0)
    my_decay = lax.dynamic_slice_in_dim(decay[:, :NOCC], time_rank * local_times, local_times, 0)
    mine = (mine.astype(jnp.float32)[:, None, :] * my_decay[None]).astype(jnp.bfloat16)
    green_slab = jnp.einsum("rti,iq->rtq", mine, psi_slab, preferred_element_type=jnp.float32)
    return green_slab * screened_time


def solution(mesh):
    in_specs = (P(), P(None, "pts"), P(), P(), P(), P("pts", None))
    out_specs = P("pts", "tm", None)
    return jax.shard_map(
        per_device, mesh=mesh, in_specs=in_specs, out_specs=out_specs, check_vma=False
    )
```

time: 386 us -> 157 us (0.41)
  waiting for transfers between devices: 304 us -> 77.3 us
  matrix products: 57.3 us -> 28.9 us
  local copies, waits for them, and re-layouts: 1.67 us -> 22.6 us
  starting transfers between devices: 0.49 us -> 6.36 us
    all_gather x2 -> x0, waiting for transfers between devices: 239 us -> none  [the longest x1 188 us: per_device(): piece = lax.all_gather(chi_time, 'tm', axis=1, tiled=True)]
    dot_general x9 -> x5, matrix products: 57.3 us -> 28.9 us  [the longest x1 15.1 us: per_device(): jnp.dot(scaled[:, NOCC:], psi_cols[NOCC:], preferred_element_type=jnp.flo...]
    reshape x0 -> x1, local copies, waits for them, and re-layouts: none -> 11 us  [per_device(): dealt = psi_rows.reshape(owners, teams, share, orbitals)]
    all_to_all x0 -> x1, waiting for transfers between devices: none -> 7.13 us  [per_device(): lax.all_to_all(by_time, 'tm', split_axis=1, concat_axis=0, tiled=True)]
    all_to_all x0 -> x1, starting transfers between devices: none -> 6.36 us  [per_device(): lax.all_to_all(by_time, 'tm', split_axis=1, concat_axis=0, tiled=True)]
    convert_element_type x1 -> x3, other arithmetic: 1.75 us -> 7.25 us  [the longest x1 4.79 us: per_device(): scaled = (dealt[:, None, :] * decay[None, :, :]).astype(jnp.bfloat16)]
    reduce_scatter x1, waiting for transfers between devices: 65.1 us -> 70.2 us  [per_device(): summed = lax.psum_scatter(partial, 'pts', scatter_dimension=0, tiled=True)]
    unnamed x16 -> x8, local copies, waits for them, and re-layouts: 0.04 us -> 4.53 us
  transfers between devices with their start and end apart: 3 -> 2, of which waited for: 3 -> 2; matrix products, arithmetic and copies ran while one was open for 1% -> 1% of each run, Pallas kernels for 0% -> 0%
where the time goes in v1:
time: 157 us; the launch traced here: 156 us
  waiting for transfers between devices  77.3 us (49%)
  matrix products  28.9 us (18%)
  local copies, waits for them, and re-layouts  22.6 us (14%)
  between operations  13.5 us (9%)
  other arithmetic  7.41 us (5%)
  starting transfers between devices  6.36 us (4%)
    reduce_scatter x1, waiting for transfers between devices, per_device(): summed = lax.psum_scatter(partial, 'pts', scatter_dimension=0, tiled=True)  70.2 us
    dot_general x1, matrix products, per_device(): jnp.dot(scaled[:, NOCC:], psi_cols[NOCC:], preferred_element_type=jnp.flo...  15.1 us
    reshape x1, local copies, waits for them, and re-layouts, per_device(): dealt = psi_rows.reshape(owners, teams, share, orbitals)  11 us
    dot_general x1, matrix products, per_device(): partial = jnp.dot(chi_time, coulomb, preferred_element_type=jnp.float32)  9.89 us
    all_to_all x1, waiting for transfers between devices, per_device(): lax.all_to_all(by_time, 'tm', split_axis=1, concat_axis=0, tiled=True)  7.13 us
    all_to_all x1, starting transfers between devices, per_device(): lax.all_to_all(by_time, 'tm', split_axis=1, concat_axis=0, tiled=True)  6.36 us
    convert_element_type x1, other arithmetic, per_device(): scaled = (dealt[:, None, :] * decay[None, :, :]).astype(jnp.bfloat16)  4.79 us
    unnamed x8, local copies, waits for them, and re-layouts  4.53 us
  transfers between devices with their start and end apart: 2, of which 2 were waited for; matrix products, arithmetic and copies ran while one was open for 1% of the time, Pallas kernels for 0%

profile of v1, /device:TPU:0, one launch (start us, length us, event | category | flops | bytes accessed | tf_op | source)
XLA Modules:
  0.0 156.1 jit_solution(5427885573996503059)
XLA Ops:
  6.5 0.0 copy-start
  6.5 0.0 reduce-scatter.2.cloned.1.call-start
  6.6 11.0 %reshape.87 = bf16[16,8,4,6144]{3,2,1,0:T(4,128)(2,1)} reshape(bf16[512,6144]{1,0:T(8,128)(2,1)} %param.6) | data formatting | bytes 12582912 | tf_op jit(solution)/shard_map/reshape | solution.py:43
  17.6 0.0 copy-start.2
  17.6 0.0 copy-start.3
  17.6 2.4 %dynamic-slice_convert_fusion = f32[16,1,4,6144]{3,2,1,0:T(4,128)} fusion(bf16[16,8,4,6144]{3,2,1,0:T(4,128)(2,1)} %reshape.87, s32[]{:T(128)S(6)} %select_n.12), kind=kLoop, calls=%fused_computation.13 | loop fusion | flops 393216 | bytes 2359300 | tf_op jit(solution)/shard_map/convert_element_type | solution.py:45
  20.0 2.8 %reshape.89 = f32[64,6144]{1,0:T(8,128)} reshape(f32[16,1,4,6144]{3,2,1,0:T(4,128)} %dynamic-slice_convert_fusion) | data formatting | bytes 3145728 | tf_op jit(solution)/shard_map/convert_element_type | solution.py:45
  22.9 0.0 copy-done.2
  22.9 0.0 copy-done.3
  22.9 0.1 multiply_exponential_fusion
  23.0 4.8 %multiply_convert_fusion = bf16[64,16,6144]{2,1,0:T(8,128)(2,1)S(1)} fusion(f32[16,6144]{1,0:T(8,128)S(1)} %multiply_exponential_fusion, f32[64,6144]{1,0:T(8,128)} %reshape.89), kind=kLoop, calls=%fused_computation | loop fusion | flops 12582912 | bytes 14548992 | tf_op jit(solution)/shard_map/convert_element_type | solution.py:48
  27.8 0.0 copy-start.1
  27.8 4.5 %copy-done.1 = bf16[64,16,6144]{2,1,0:T(8,128)(2,1)} copy-done((bf16[64,16,6144]{2,1,0:T(8,128)(2,1)}, bf16[64,16,6144]{2,1,0:T(8,128)(2,1)S(1)}, u32[]{:S(2)}) %copy-start.1) | copy-done | bytes 12582936
  32.3 15.1 %fusion = f32[1024,1024]{1,0:T(8,128)} fusion(bf16[1024,6144]{1,0:T(8,128)(2,1)S(1)} %bitcast.25, bf16[6144,1024]{1,0:T(8,128)(2,1)} %param.7), kind=kOutput, calls=%fused_computation.1 | convolution fusion | flops 10737418240 | bytes 25165824 | tf_op jit(solution)/shard_map/dot_general | solution.py:51
  47.4 0.0 copy-done
  47.4 9.9 %fusion.12 = f32[1024,1024]{1,0:T(8,128)} fusion(bf16[1024,1024]{1,0:T(8,128)(2,1)S(1)} %copy-done, f32[1024,1024]{1,0:T(8,128)} %fusion, bf16[1024,6144]{1,0:T(8,128)(2,1)} %bitcast.26, bf16[6144,1024]{1,0:T(8,128)(2,1)} %param.7), kind=kOutput, calls=%fused_computation.12 | convolution fusion | flops 4297064448 | bytes 14680064 | tf_op jit(solution)/shard_map/dot_general | solution.py:53
  57.3 0.0 slice-start
  57.3 0.0 reduce-scatter.2.cloned.1.call-update
  57.4 70.2 %reduce-scatter.2.cloned.1.call-done = f32[64,1024]{1,0:T(8,128)} async-done(((f32[1024,1024]{1,0:T(8,128)}), f32[64,1024]{1,0:T(8,128)}) %reduce-scatter.2.cloned.1.call-update) | async-done | bytes 262160 | tf_op jit(solution)/shard_map/reduce_scatter | solution.py:54
  127.6 1.4 convolution_bitcast_fusion.1
  129.0 0.5 convolution_bitcast_fusion
  129.5 0.9 copy.9
  130.3 6.4 %all-to-all-start = ((f32[4,16,1024]{2,0,1:T(4,128)}), f32[4,16,1024]{2,0,1:T(4,128)}, u32[]{:S(2)}, u32[]{:S(2)}) async-start(f32[4,16,1024]{2,0,1:T(4,128)} %copy.9), calls=%async_computation.1 | async-start | bytes 524288 | tf_op jit(solution)/shard_map/all_to_all | solution.py:60
  136.7 0.6 slice.24
  137.3 0.8 constant_dynamic-slice_fusion
  138.1 0.0 slice-done
  138.1 7.1 %all-to-all-done = f32[4,16,1024]{2,0,1:T(4,128)} async-done(((f32[4,16,1024]{2,0,1:T(4,128)}), f32[4,16,1024]{2,0,1:T(4,128)}, u32[]{:S(2)}, u32[]{:S(2)}) %all-to-all-start) | async-done | bytes 262176 | tf_op jit(solution)/shard_map/all_to_all | solution.py:60
  145.2 1.0 copy.13
  146.2 0.1 all_to_all.16
  146.3 2.1 %fusion.7 = f32[32,2,1024]{2,0,1:T(8,128)S(1)} fusion(f32[32,2,1024]{2,0,1:T(8,128)S(1)} %all_to_all.16, bf16[1024,1024]{1,0:T(8,128)(2,1)} %param.8, f32[2,1024]{1,0:T(2,128)S(1)} %constant_dynamic-slice_fusion, f32[32,1024]{1,0:T(8,128)S(1)} %dynamic-slice_convert_fusion.1), kind=kOutput, calls=%fused_computation.9 | convolution fusion | flops 134414336 | bytes 2760704 | tf_op jit(solution)/shard_map/rti,iq->rtq/dot_general | solution.py:65
  148.4 0.9 copy.11
  (5 shorter events, 0.0 us)
Async XLA Ops:
  6.5 40.9 %copy-start = (bf16[1024,1024]{1,0:T(8,128)(2,1)S(1)}, bf16[1024,1024]{1,0:T(8,128)(2,1)}, u32[]{:S(2)}) copy-start(bf16[1024,1024]{1,0:T(8,128)(2,1)} %param.11) | copy-start | bytes 6291460
  6.5 121.0 %reduce-scatter.2.cloned.1.call-start = ((), (), s32[]{:S(2)}) async-start(), calls=%async_computation.2 | async-start | bytes 4456448 | tf_op jit(solution)/shard_map/reduce_scatter | solution.py:54
  17.6 5.3 %copy-start.2 = (f32[5120]{0:T(1024)S(1)}, f32[5120]{0:T(1024)}, u32[]{:S(2)}) copy-start(f32[5120]{0:T(1024)} %param.10) | copy-start | bytes 61444
  17.6 5.3 %copy-start.3 = (f32[1024]{0:T(1024)S(1)}, f32[1024]{0:T(1024)}, u32[]{:S(2)}) copy-start(f32[1024]{0:T(1024)} %param.9) | copy-start | bytes 12292
  27.8 4.5 %copy-start.1 = (bf16[64,16,6144]{2,1,0:T(8,128)(2,1)}, bf16[64,16,6144]{2,1,0:T(8,128)(2,1)S(1)}, u32[]{:S(2)}) copy-start(bf16[64,16,6144]{2,1,0:T(8,128)(2,1)S(1)} %multiply_convert_fusion) | copy-start | bytes 37748740
  57.3 80.7 %slice-start = ((bf16[512,6144]{1,0:T(8,128)(2,1)}), bf16[512,1024]{1,0:T(8,128)(2,1)S(1)}, s32[]{:S(2)}) async-start(bf16[512,6144]{1,0:T(8,128)(2,1)} %param.6), calls=%async_computation.3 | async-start | bytes 2097152 | tf_op jit(solution)/shard_map/slice | solution.py:62
  130.3 14.9 %all-to-all-start = ((f32[4,16,1024]{2,0,1:T(4,128)}), f32[4,16,1024]{2,0,1:T(4,128)}, u32[]{:S(2)}, u32[]{:S(2)}) async-start(f32[4,16,1024]{2,0,1:T(4,128)} %copy.9), calls=%async_computation.1 | async-start | bytes 524288 | tf_op jit(solution)/shard_map/all_to_all | solution.py:60
Sparse Core Ops, SparseCore 0:
  57.5 70.0 reduce-scatter.1

commit v2 on v1

v2 whole, which is shorter than its diff:
```python
import functools
import math

import jax
import jax.numpy as jnp
import ml_dtypes
import numpy as np
from jax import lax
from jax.experimental import pallas as pl
from jax.experimental.pallas import tpu as pltpu
from jax.sharding import PartitionSpec as P

MESH = pl.DeviceIdType.MESH
NOCC = 1024
TIMES = 16
TIME_SPAN = 8.0
FREQ_SPAN = 8.0
TILE = 256
CORES = 2


def transform_tables():
    fraction = (np.arange(TIMES, dtype=np.float64) + 0.5) / TIMES
    times_grid = TIME_SPAN * fraction * fraction
    time_weight = TIME_SPAN * 2.0 * fraction / TIMES
    frequency = FREQ_SPAN * fraction * fraction
    freq_weight = FREQ_SPAN * 2.0 * fraction / TIMES
    forward = time_weight[None, :] * np.cos(frequency[:, None] * times_grid[None, :])
    backward = (
        2.0 / math.pi * freq_weight[None, :] * np.cos(times_grid[:, None] * frequency[None, :])
    )
    return forward.astype(np.float32), backward.astype(np.float32)


def forward_blocks(groups):
    forward, _ = transform_tables()
    whole = np.kron(np.eye(groups, dtype=np.float32), forward)
    high = whole.astype(ml_dtypes.bfloat16)
    low = (whole - high.astype(np.float32)).astype(ml_dtypes.bfloat16)
    return np.stack([high, low])


def kernel(
    sizes,
    rows_hbm, cols_hbm, slab_hbm, occ_ref, virt_ref, coulomb_hbm, forward_ref, backward_ref,
    out_hbm,
    raw, rows, decay, scaled0, scaled1, own_scaled, cols, coulomb, slab, chi, freq,
    half, half_send, half_recv, sum_send, sum_recv, mine, green, sigma,
    raw_sem, cols_sem, misc_sem, half_ssem, half_rsem, sum_ssem, sum_rsem, out_ssem, out_rsem,
    own_sem,
):
    teams, zs, ys, share, band = sizes
    owners = zs * ys * CORES
    peers = zs * ys
    tiles = cols.shape[0]
    orbitals = decay.shape[1]
    chunk = owners * TIMES
    halves = chunk // CORES
    strip = orbitals // tiles
    t = lax.axis_index("tm")
    p = lax.axis_index("pts")
    core = lax.rem(p, CORES)
    y = lax.rem(p // CORES, ys)
    z = p // (CORES * ys)
    partner = (t, p + 1 - 2 * core)

    def peer(h):
        return lax.rem(z + h // ys, zs), lax.rem(y + h % ys, ys)

    def peer_id(h):
        pz, py = peer(h)
        return (t, (pz * ys + py) * CORES + core)

    def team_id(d):
        return (lax.rem(t + d, teams), p)

    barrier = pltpu.get_barrier_semaphore()
    pl.semaphore_signal(barrier, inc=1, device_id=partner, device_id_type=MESH)
    for h in range(1, peers):
        pl.semaphore_signal(barrier, inc=1, device_id=peer_id(h), device_id_type=MESH)
    for d in range(1, teams):
        pl.semaphore_signal(barrier, inc=1, device_id=team_id(d), device_id_type=MESH)

    def raw_copy(g):
        owner = (g % peers) * CORES + g // peers
        first = pl.multiple_of(owner * (teams * share) + (t * share) // band * band, band)
        return pltpu.make_async_copy(
            rows_hbm.at[pl.ds(first, band)], raw.at[pl.ds(g * band, band)], raw_sem.at[g]
        )

    def cols_copy(n):
        return pltpu.make_async_copy(
            cols_hbm.at[:, pl.ds(pl.multiple_of(n * TILE, TILE), TILE)], cols.at[n], cols_sem.at[n]
        )

    for g in range(owners):
        raw_copy(g).start()
    for n in range(tiles):
        cols_copy(n).start()
    coulomb_copy = pltpu.make_async_copy(coulomb_hbm, coulomb, misc_sem.at[0])
    slab_copy = pltpu.make_async_copy(slab_hbm, slab, misc_sem.at[1])
    coulomb_copy.start()
    slab_copy.start()

    fraction = (lax.broadcasted_iota(jnp.int32, (TIMES, 1), 0).astype(jnp.float32) + 0.5) / TIMES
    moments = TIME_SPAN * fraction * fraction
    decay[:, :NOCC] = jnp.exp(-occ_ref[...] * moments)
    decay[:, NOCC:] = jnp.exp(-virt_ref[...] * moments)
    for g in range(owners):
        raw_copy(g).wait()
    rows[...] = raw[...].astype(jnp.float32)
    inner = lax.rem(t * share, band)

    def scale(target, s, n):
        where = pl.ds(pl.multiple_of(n * strip, strip), strip)
        factor = decay[:, where]
        for g in range(owners):
            row = rows[pl.ds(g * band + inner + s, 1), where]
            target[g * TIMES : (g + 1) * TIMES, where] = (row * factor).astype(jnp.bfloat16)

    scaled = (scaled0, scaled1)
    own_group = core * peers + z * ys + y
    for s in range(share):
        row = rows[pl.ds(own_group * band + inner + s, 1), :NOCC]
        own_scaled[s * TIMES : (s + 1) * TIMES] = (row * decay[:, :NOCC]).astype(jnp.bfloat16)

    def first_scale(n, carry):
        scale(scaled0, 0, n)
        return carry

    lax.fori_loop(0, tiles, first_scale, 0)

    def half_copy(s):
        return pltpu.make_async_remote_copy(
            half_send.at[s], half_recv.at[s], half_ssem.at[s], half_rsem.at[s],
            device_id=partner, device_id_type=MESH,
        )

    def sum_copy(s, h):
        pz, py = peer(h)
        where = pl.ds(pl.multiple_of((pz * ys + py) * TIMES, TIMES), TIMES)
        return pltpu.make_async_remote_copy(
            sum_send.at[s, where], sum_recv.at[s, h - 1], sum_ssem.at[s, h - 1],
            sum_rsem.at[s, h - 1], device_id=peer_id(h), device_id_type=MESH,
        )

    def out_copy(s, d):
        return pltpu.make_async_remote_copy(
            sigma.at[s, lax.rem(t + d, teams)], out_hbm.at[t * share + s],
            out_ssem.at[s, d - 1], out_rsem.at[s, d - 1],
            device_id=team_id(d), device_id_type=MESH,
        )

    def own_copy(s):
        return pltpu.make_async_copy(sigma.at[s, t], out_hbm.at[t * share + s], own_sem.at[s])

    def green_loop(s):
        now, later = scaled[s % 2], scaled[(s + 1) % 2]

        def body(n, carry):
            if s == 0:
                cols_copy(n).wait()
            occ = jnp.dot(now[:, :NOCC], cols[n, :NOCC], preferred_element_type=jnp.float32)
            virt = jnp.dot(now[:, NOCC:], cols[n, NOCC:], preferred_element_type=jnp.float32)
            where = pl.ds(pl.multiple_of(n * TILE, TILE), TILE)
            chi[:, where] = (occ * virt).astype(jnp.bfloat16)
            if s + 1 < share:
                scale(later, s + 1, n)
            return carry

        lax.fori_loop(0, tiles, body, 0)

    def screen(s):
        def to_freq(n, carry):
            where = pl.ds(pl.multiple_of(n * TILE, TILE), TILE)
            part = chi[:, where]
            freq[:, where] = (
                jnp.dot(forward_ref[0], part, preferred_element_type=jnp.float32)
                + jnp.dot(forward_ref[1], part, preferred_element_type=jnp.float32)
            ).astype(jnp.bfloat16)
            return carry

        lax.fori_loop(0, chi.shape[1] // TILE, to_freq, 0)
        if s == 0:
            coulomb_copy.wait()
        theirs = pl.ds(pl.multiple_of((1 - core) * halves, halves), halves)
        ours = pl.ds(pl.multiple_of(core * halves, halves), halves)

        def send_part(n, carry):
            where = pl.ds(pl.multiple_of(n * TILE, TILE), TILE)
            half_send[s, :, where] = jnp.dot(
                freq[theirs, :], coulomb[:, where], preferred_element_type=jnp.float32
            ).astype(jnp.bfloat16)
            return carry

        def keep_part(n, carry):
            where = pl.ds(pl.multiple_of(n * TILE, TILE), TILE)
            half[:, where] = jnp.dot(
                freq[ours, :], coulomb[:, where], preferred_element_type=jnp.float32
            )
            return carry

        lax.fori_loop(0, coulomb.shape[1] // TILE, send_part, 0)
        if s == 0:
            pl.semaphore_wait(barrier, 1 + (peers - 1) + (teams - 1))
        half_copy(s).start()
        lax.fori_loop(0, coulomb.shape[1] // TILE, keep_part, 0)

    def pair_up(s):
        half_copy(s).wait_recv()
        sum_send[s] = (half[...] + half_recv[s].astype(jnp.float32)).astype(jnp.bfloat16)
        for h in range(peers - 1, 0, -1):
            sum_copy(s, h).start()
        here = pl.ds(pl.multiple_of((z * ys + y) * TIMES, TIMES), TIMES)
        mine[s] = half[here, :] + half_recv[s, here, :].astype(jnp.float32)

    def finish(s):
        total = mine[s]
        for h in range(1, peers):
            sum_copy(s, h).wait_recv()
        for h in range(1, peers):
            total = total + sum_recv[s, h - 1].astype(jnp.float32)
        resummed = total / jnp.sqrt(1.0 + total * total)
        by_time = jnp.dot(
            backward_ref[...], resummed, preferred_element_type=jnp.float32,
            precision=lax.Precision.HIGHEST,
        )
        result = by_time * green[s * TIMES : (s + 1) * TIMES]
        local = TIMES // teams
        for d in range(teams):
            sigma[s, d] = result[d * local : (d + 1) * local]
        for d in range(teams - 1, 0, -1):
            out_copy(s, d).start()
        own_copy(s).start()

    for s in range(share):
        green_loop(s)
        if s > 0:
            pair_up(s - 1)
        screen(s)
    pair_up(share - 1)
    slab_copy.wait()
    green[...] = jnp.dot(own_scaled[...], slab[...], preferred_element_type=jnp.float32)
    for s in range(share):
        finish(s)
    for s in range(share):
        half_copy(s).wait_send()
        for h in range(1, peers):
            sum_copy(s, h).wait_send()
        own_copy(s).wait()
        for d in range(1, teams):
            out_copy(s, d).wait_send()
            out_copy(s, d).wait_recv()


def per_device(sizes, psi_rows, psi_cols, psi_slab, occ_depth, virt_height, coulomb):
    teams, zs, ys, share, band = sizes
    owners = zs * ys * CORES
    peers = zs * ys
    orbitals = psi_rows.shape[1]
    points = psi_cols.shape[1]
    slab = psi_slab.shape[1]
    chunk = owners * TIMES
    halves = chunk // CORES
    _, backward = transform_tables()
    bf16, f32 = jnp.bfloat16, jnp.float32
    anywhere = pl.BlockSpec(memory_space=pl.ANY)
    inside = pl.BlockSpec(memory_space=pltpu.VMEM)
    dma = pltpu.SemaphoreType.DMA
    return pl.pallas_call(
        functools.partial(kernel, sizes),
        name="gw_window",
        out_shape=jax.ShapeDtypeStruct((teams * share, TIMES // teams, slab), f32),
        in_specs=[anywhere, anywhere, anywhere, inside, inside, anywhere, inside, inside],
        out_specs=anywhere,
        scratch_shapes=[
            pltpu.VMEM((owners * band, orbitals), bf16),
            pltpu.VMEM((owners * band, orbitals), f32),
            pltpu.VMEM((TIMES, orbitals), f32),
            pltpu.VMEM((chunk, orbitals), bf16),
            pltpu.VMEM((chunk, orbitals), bf16),
            pltpu.VMEM((share * TIMES, NOCC), bf16),
            pltpu.VMEM((points // TILE, orbitals, TILE), bf16),
            pltpu.VMEM((points, slab), bf16),
            pltpu.VMEM((NOCC, slab), bf16),
            pltpu.VMEM((chunk, points), bf16),
            pltpu.VMEM((chunk, points), bf16),
            pltpu.VMEM((halves, slab), f32),
            pltpu.VMEM((share, halves, slab), bf16),
            pltpu.VMEM((share, halves, slab), bf16),
            pltpu.VMEM((share, halves, slab), bf16),
            pltpu.VMEM((share, peers - 1, TIMES, slab), bf16),
            pltpu.VMEM((share, TIMES, slab), f32),
            pltpu.VMEM((share * TIMES, slab), f32),
            pltpu.VMEM((share, teams, TIMES // teams, slab), f32),
            dma((owners,)),
            dma((points // TILE,)),
            dma((2,)),
            dma((share,)),
            dma((share,)),
            dma((share, peers - 1)),
            dma((share, peers - 1)),
            dma((share, teams - 1)),
            dma((share, teams - 1)),
            dma((share,)),
        ],
        compiler_params=pltpu.CompilerParams(
            collective_id=0, has_side_effects=True, vmem_limit_bytes=60 * 1024 * 1024
        ),
    )(
        psi_rows, psi_cols, psi_slab, occ_depth[None], virt_height[None], coulomb,
        jnp.asarray(forward_blocks(owners)), jnp.asarray(backward),
    )


def solution(mesh):
    teams, owners = mesh.shape["tm"], mesh.shape["pts"]
    ys = owners // (2 * CORES)
    sizes = (teams, 2, ys, 512 // (owners * teams), 8)
    in_specs = (P(), P(None, "pts"), P(), P(), P(), P("pts", None))
    out_specs = P("pts", "tm", None)
    return jax.shard_map(
        functools.partial(per_device, sizes),
        mesh=mesh, in_specs=in_specs, out_specs=out_specs, check_vma=False,
    )
```

time: 157 us -> 54.9 us (0.35)
  waiting for transfers between devices: 77.3 us -> 0 us
  Pallas kernels: 0 us -> 53.1 us
  matrix products: 28.9 us -> 0 us
  local copies, waits for them, and re-layouts: 22.6 us -> 1.67 us
  between operations: 13.5 us -> 0.01 us
  other arithmetic: 7.41 us -> 0 us
  starting transfers between devices: 6.36 us -> 0 us
    reduce_scatter x1 -> x0, waiting for transfers between devices: 70.2 us -> none  [per_device(): summed = lax.psum_scatter(partial, 'pts', scatter_dimension=0, tiled=True)]
    pallas_call x0 -> x1, Pallas kernels: none -> 53.1 us  [per_device(): pl.pallas_call(functools.partial(kernel, sizes), name='gw_window', out_sh...]
    dot_general x5 -> x0, matrix products: 28.9 us -> none  [the longest x1 15.1 us: per_device(): jnp.dot(scaled[:, NOCC:], psi_cols[NOCC:], preferred_element_type=jnp.flo...]
    reshape x1 -> x0, local copies, waits for them, and re-layouts: 11 us -> none  [per_device(): dealt = psi_rows.reshape(owners, teams, share, orbitals)]
    convert_element_type x3 -> x0, other arithmetic: 7.25 us -> none  [the longest x1 4.79 us: per_device(): scaled = (dealt[:, None, :] * decay[None, :, :]).astype(jnp.bfloat16)]
    all_to_all x1 -> x0, waiting for transfers between devices: 7.13 us -> none  [per_device(): lax.all_to_all(by_time, 'tm', split_axis=1, concat_axis=0, tiled=True)]
    all_to_all x1 -> x0, starting transfers between devices: 6.36 us -> none  [per_device(): lax.all_to_all(by_time, 'tm', split_axis=1, concat_axis=0, tiled=True)]
    unnamed x8 -> x1, local copies, waits for them, and re-layouts: 4.53 us -> 1.67 us
  transfers between devices with their start and end apart: 2 -> 0, of which waited for: 2 -> 0; matrix products, arithmetic and copies ran while one was open for 1% -> 0% of each run, Pallas kernels for 0% -> 0%
where the time goes in v2:
time: 54.9 us; the launch traced here: 54.8 us
  Pallas kernels  53.1 us (97%)
  local copies, waits for them, and re-layouts  1.67 us (3%)
    pallas_call x1, Pallas kernels, per_device(): pl.pallas_call(functools.partial(kernel, sizes), name='gw_window', out_sh...  53.1 us
    unnamed x1, local copies, waits for them, and re-layouts  1.67 us

profile of v2, /device:TPU:0, one launch (start us, length us, event | category | flops | bytes accessed | tf_op | source)
XLA Modules:
  0.0 54.8 jit_solution(11200924864266782555)
XLA Ops:
  0.0 53.1 %gw_window.1 = f32[32,2,1024]{2,1,0:T(2,128)} custom-call(bf16[512,6144]{1,0:T(8,128)(2,1)} %rows_hbm.1, bf16[6144,1024]{1,0:T(8,128)(2,1)} %cols_hbm.1, bf16[1024,1024]{1,0:T(8,128)(2,1)} %slab_hbm.1, f32[1,1024]{1,0:T(1,128)} %bitcast.3, f32[1,5120]{1,0:T(1,128)} %bitcast.2, bf16[1024,1024]{1,0:T(8,128)(2,1)} %coulomb_hbm.1, ...), custom_call_target="tpu_custom_call" | custom-call | tf_op jit(solution)/shard_map/gw_window/pallas_call | solution.py:270
  53.1 1.7 %copy.10 = f32[32,2,1024]{2,1,0:T(2,128)} copy(f32[32,2,1024]{2,1,0:T(2,128)} %gw_window.1) | data formatting | bytes 524288

commit v3 on v2

--- a/solution.py
+++ b/solution.py
@@ -37,7 +37,7 @@
     whole = np.kron(np.eye(groups, dtype=np.float32), forward)
     high = whole.astype(ml_dtypes.bfloat16)
     low = (whole - high.astype(np.float32)).astype(ml_dtypes.bfloat16)
-    return np.stack([high, low])
+    return np.concatenate([high, low], axis=1)
 
 
 def kernel(
@@ -82,7 +82,8 @@
         pl.semaphore_signal(barrier, inc=1, device_id=team_id(d), device_id_type=MESH)
 
     def raw_copy(g):
-        owner = (g % peers) * CORES + g // peers
+        pz, py = peer(g % peers)
+        owner = (pz * ys + py) * CORES + (1 - core if g < peers else core)
         first = pl.multiple_of(owner * (teams * share) + (t * share) // band * band, band)
         return pltpu.make_async_copy(
             rows_hbm.at[pl.ds(first, band)], raw.at[pl.ds(g * band, band)], raw_sem.at[g]
@@ -119,7 +120,7 @@
             target[g * TIMES : (g + 1) * TIMES, where] = (row * factor).astype(jnp.bfloat16)
 
     scaled = (scaled0, scaled1)
-    own_group = core * peers + z * ys + y
+    own_group = peers
     for s in range(share):
         row = rows[pl.ds(own_group * band + inner + s, 1), :NOCC]
         own_scaled[s * TIMES : (s + 1) * TIMES] = (row * decay[:, :NOCC]).astype(jnp.bfloat16)
@@ -137,10 +138,8 @@
         )
 
     def sum_copy(s, h):
-        pz, py = peer(h)
-        where = pl.ds(pl.multiple_of((pz * ys + py) * TIMES, TIMES), TIMES)
         return pltpu.make_async_remote_copy(
-            sum_send.at[s, where], sum_recv.at[s, h - 1], sum_ssem.at[s, h - 1],
+            sum_send.at[s, pl.ds(h * TIMES, TIMES)], sum_recv.at[s, h - 1], sum_ssem.at[s, h - 1],
             sum_rsem.at[s, h - 1], device_id=peer_id(h), device_id_type=MESH,
         )
 
@@ -154,7 +153,7 @@
     def own_copy(s):
         return pltpu.make_async_copy(sigma.at[s, t], out_hbm.at[t * share + s], own_sem.at[s])
 
-    def green_loop(s):
+    def green_loop(s, between):
         now, later = scaled[s % 2], scaled[(s + 1) % 2]
 
         def body(n, carry):
@@ -166,58 +165,48 @@
             chi[:, where] = (occ * virt).astype(jnp.bfloat16)
             if s + 1 < share:
                 scale(later, s + 1, n)
+            for after, work in between.items():
+                pl.when(n == after)(work)
             return carry
 
         lax.fori_loop(0, tiles, body, 0)
 
     def screen(s):
-        def to_freq(n, carry):
-            where = pl.ds(pl.multiple_of(n * TILE, TILE), TILE)
-            part = chi[:, where]
-            freq[:, where] = (
-                jnp.dot(forward_ref[0], part, preferred_element_type=jnp.float32)
-                + jnp.dot(forward_ref[1], part, preferred_element_type=jnp.float32)
-            ).astype(jnp.bfloat16)
-            return carry
-
-        lax.fori_loop(0, chi.shape[1] // TILE, to_freq, 0)
+        for n in range(chi.shape[1] // TILE):
+            where = slice(n * TILE, (n + 1) * TILE)
+            for part in range(CORES):
+                group = slice(part * halves, (part + 1) * halves)
+                twice = jnp.concatenate([chi[group, where]] * 2, axis=0)
+                freq[group, where] = jnp.dot(
+                    forward_ref[...], twice, preferred_element_type=jnp.float32
+                ).astype(jnp.bfloat16)
         if s == 0:
             coulomb_copy.wait()
-        theirs = pl.ds(pl.multiple_of((1 - core) * halves, halves), halves)
-        ours = pl.ds(pl.multiple_of(core * halves, halves), halves)
-
-        def send_part(n, carry):
-            where = pl.ds(pl.multiple_of(n * TILE, TILE), TILE)
-            half_send[s, :, where] = jnp.dot(
-                freq[theirs, :], coulomb[:, where], preferred_element_type=jnp.float32
-            ).astype(jnp.bfloat16)
-            return carry
-
-        def keep_part(n, carry):
-            where = pl.ds(pl.multiple_of(n * TILE, TILE), TILE)
-            half[:, where] = jnp.dot(
-                freq[ours, :], coulomb[:, where], preferred_element_type=jnp.float32
-            )
-            return carry
-
-        lax.fori_loop(0, coulomb.shape[1] // TILE, send_part, 0)
+        for n in range(coulomb.shape[1] // TILE):
+            where = slice(n * TILE, (n + 1) * TILE)
+            part = jnp.dot(freq[...], coulomb[:, where], preferred_element_type=jnp.float32)
+            half_send[s, :, where] = part[:halves].astype(jnp.bfloat16)
+            half[:, where] = part[halves:]
         if s == 0:
             pl.semaphore_wait(barrier, 1 + (peers - 1) + (teams - 1))
         half_copy(s).start()
-        lax.fori_loop(0, coulomb.shape[1] // TILE, keep_part, 0)
 
     def pair_up(s):
         half_copy(s).wait_recv()
-        sum_send[s] = (half[...] + half_recv[s].astype(jnp.float32)).astype(jnp.bfloat16)
+        total = half[...] + half_recv[s].astype(jnp.float32)
+        sum_send[s] = total.astype(jnp.bfloat16)
+        mine[s] = total[:TIMES]
         for h in range(peers - 1, 0, -1):
             sum_copy(s, h).start()
-        here = pl.ds(pl.multiple_of((z * ys + y) * TIMES, TIMES), TIMES)
-        mine[s] = half[here, :] + half_recv[s, here, :].astype(jnp.float32)
+
+    def slab_part():
+        slab_copy.wait()
+        green[...] = jnp.dot(own_scaled[...], slab[...], preferred_element_type=jnp.float32)
 
     def finish(s):
-        total = mine[s]
         for h in range(1, peers):
             sum_copy(s, h).wait_recv()
+        total = mine[s]
         for h in range(1, peers):
             total = total + sum_recv[s, h - 1].astype(jnp.float32)
         resummed = total / jnp.sqrt(1.0 + total * total)
@@ -234,14 +223,17 @@
         own_copy(s).start()
 
     for s in range(share):
-        green_loop(s)
+        between = {}
         if s > 0:
-            pair_up(s - 1)
+            between[0] = functools.partial(pair_up, s - 1)
+        if s > 1:
+            between[1] = functools.partial(finish, s - 2)
+        green_loop(s, between)
+        if s == 0:
+            slab_part()
         screen(s)
     pair_up(share - 1)
-    slab_copy.wait()
-    green[...] = jnp.dot(own_scaled[...], slab[...], preferred_element_type=jnp.float32)
-    for s in range(share):
+    for s in range(max(share - 2, 0), share):
         finish(s)
     for s in range(share):
         half_copy(s).wait_send()
@@ -309,7 +301,7 @@
         ),
     )(
         psi_rows, psi_cols, psi_slab, occ_depth[None], virt_height[None], coulomb,
-        jnp.asarray(forward_blocks(owners)), jnp.asarray(backward),
+        jnp.asarray(forward_blocks(peers)), jnp.asarray(backward),
     )
 
 

time: 54.9 us -> 48.6 us (0.89)
  Pallas kernels: 53.1 us -> 46.8 us
    pallas_call x1, Pallas kernels: 53.1 us -> 46.8 us  [per_device(): pl.pallas_call(functools.partial(kernel, sizes), name='gw_window', out_sh...]
where the time goes in v3:
time: 48.6 us; the launch traced here: 48.4 us
  Pallas kernels  46.8 us (96%)
  local copies, waits for them, and re-layouts  1.67 us (3%)
    pallas_call x1, Pallas kernels, per_device(): pl.pallas_call(functools.partial(kernel, sizes), name='gw_window', out_sh...  46.8 us
    unnamed x1, local copies, waits for them, and re-layouts  1.67 us

profile of v3, /device:TPU:0, one launch (start us, length us, event | category | flops | bytes accessed | tf_op | source)
XLA Modules:
  0.0 48.4 jit_solution(5575782078751754157)
XLA Ops:
  0.0 46.8 %gw_window.1 = f32[32,2,1024]{2,1,0:T(2,128)} custom-call(bf16[512,6144]{1,0:T(8,128)(2,1)} %rows_hbm.1, bf16[6144,1024]{1,0:T(8,128)(2,1)} %cols_hbm.1, bf16[1024,1024]{1,0:T(8,128)(2,1)} %slab_hbm.1, f32[1,1024]{1,0:T(1,128)} %bitcast.3, f32[1,5120]{1,0:T(1,128)} %bitcast.2, bf16[1024,1024]{1,0:T(8,128)(2,1)} %coulomb_hbm.1, ...), custom_call_target="tpu_custom_call" | custom-call | tf_op jit(solution)/shard_map/gw_window/pallas_call | solution.py:262
  46.8 1.7 %copy.10 = f32[32,2,1024]{2,1,0:T(2,128)} copy(f32[32,2,1024]{2,1,0:T(2,128)} %gw_window.1) | data formatting | bytes 524288

commit v4 on v3

--- a/solution.py
+++ b/solution.py
@@ -42,10 +42,10 @@
 
 def kernel(
     sizes,
-    rows_hbm, cols_hbm, slab_hbm, occ_ref, virt_ref, coulomb_hbm, forward_ref, backward_ref,
+    rows_hbm, cols_hbm, slab_hbm, occ_hbm, virt_hbm, coulomb_hbm, forward_hbm, backward_hbm,
     out_hbm,
     raw, rows, decay, scaled0, scaled1, own_scaled, cols, coulomb, slab, chi, freq,
-    half, half_send, half_recv, sum_send, sum_recv, mine, green, sigma,
+    half, half_send, half_recv, sum_send, sum_recv, mine, green, sigma, depth, forward, backward,
     raw_sem, cols_sem, misc_sem, half_ssem, half_rsem, sum_ssem, sum_rsem, out_ssem, out_rsem,
     own_sem,
 ):
@@ -94,21 +94,28 @@
             cols_hbm.at[:, pl.ds(pl.multiple_of(n * TILE, TILE), TILE)], cols.at[n], cols_sem.at[n]
         )
 
+    small_copies = [
+        pltpu.make_async_copy(occ_hbm, depth.at[:, pl.ds(0, NOCC)], misc_sem.at[2]),
+        pltpu.make_async_copy(virt_hbm, depth.at[:, pl.ds(NOCC, orbitals - NOCC)], misc_sem.at[3]),
+        pltpu.make_async_copy(forward_hbm, forward, misc_sem.at[4]),
+        pltpu.make_async_copy(backward_hbm, backward, misc_sem.at[5]),
+    ]
+    for copy in small_copies:
+        copy.start()
     for g in range(owners):
         raw_copy(g).start()
-    for n in range(tiles):
-        cols_copy(n).start()
+    cols_copy(0).start()
     coulomb_copy = pltpu.make_async_copy(coulomb_hbm, coulomb, misc_sem.at[0])
     slab_copy = pltpu.make_async_copy(slab_hbm, slab, misc_sem.at[1])
-    coulomb_copy.start()
-    slab_copy.start()
 
     fraction = (lax.broadcasted_iota(jnp.int32, (TIMES, 1), 0).astype(jnp.float32) + 0.5) / TIMES
     moments = TIME_SPAN * fraction * fraction
-    decay[:, :NOCC] = jnp.exp(-occ_ref[...] * moments)
-    decay[:, NOCC:] = jnp.exp(-virt_ref[...] * moments)
+    for copy in small_copies:
+        copy.wait()
+    decay[...] = jnp.exp(-depth[...] * moments)
     for g in range(owners):
         raw_copy(g).wait()
+    cols_copy(1).start()
     rows[...] = raw[...].astype(jnp.float32)
     inner = lax.rem(t * share, band)
 
@@ -120,11 +127,6 @@
             target[g * TIMES : (g + 1) * TIMES, where] = (row * factor).astype(jnp.bfloat16)
 
     scaled = (scaled0, scaled1)
-    own_group = peers
-    for s in range(share):
-        row = rows[pl.ds(own_group * band + inner + s, 1), :NOCC]
-        own_scaled[s * TIMES : (s + 1) * TIMES] = (row * decay[:, :NOCC]).astype(jnp.bfloat16)
-
     def first_scale(n, carry):
         scale(scaled0, 0, n)
         return carry
@@ -153,23 +155,40 @@
     def own_copy(s):
         return pltpu.make_async_copy(sigma.at[s, t], out_hbm.at[t * share + s], own_sem.at[s])
 
-    def green_loop(s, between):
+    def green_tile(now, n):
+        occ = jnp.dot(now[:, :NOCC], cols[n, :NOCC], preferred_element_type=jnp.float32)
+        virt = jnp.dot(now[:, NOCC:], cols[n, NOCC:], preferred_element_type=jnp.float32)
+        where = pl.ds(pl.multiple_of(n * TILE, TILE), TILE)
+        chi[:, where] = (occ * virt).astype(jnp.bfloat16)
+
+    def first_green():
+        def body(n, carry):
+            cols_copy(n).wait()
+
+            @pl.when(n + 2 < tiles)
+            def _():
+                cols_copy(n + 2).start()
+
+            pl.when(n == tiles - 2)(coulomb_copy.start)
+            pl.when(n == tiles - 1)(slab_copy.start)
+            green_tile(scaled0, n)
+            scale(scaled1, 1, n)
+            return carry
+
+        lax.fori_loop(0, tiles, body, 0)
+
+    def green_loop(s):
         now, later = scaled[s % 2], scaled[(s + 1) % 2]
 
-        def body(n, carry):
-            if s == 0:
-                cols_copy(n).wait()
-            occ = jnp.dot(now[:, :NOCC], cols[n, :NOCC], preferred_element_type=jnp.float32)
-            virt = jnp.dot(now[:, NOCC:], cols[n, NOCC:], preferred_element_type=jnp.float32)
-            where = pl.ds(pl.multiple_of(n * TILE, TILE), TILE)
-            chi[:, where] = (occ * virt).astype(jnp.bfloat16)
-            if s + 1 < share:
-                scale(later, s + 1, n)
-            for after, work in between.items():
-                pl.when(n == after)(work)
+        def body(pair, carry):
+            for n in (2 * pair, 2 * pair + 1):
+                green_tile(now, n)
+                if s + 1 < share:
+                    scale(later, s + 1, n)
+            pl.when(pair == 0)(functools.partial(pair_up, s - 1))
             return carry
 
-        lax.fori_loop(0, tiles, body, 0)
+        lax.fori_loop(0, tiles // 2, body, 0)
 
     def screen(s):
         for n in range(chi.shape[1] // TILE):
@@ -178,7 +197,7 @@
                 group = slice(part * halves, (part + 1) * halves)
                 twice = jnp.concatenate([chi[group, where]] * 2, axis=0)
                 freq[group, where] = jnp.dot(
-                    forward_ref[...], twice, preferred_element_type=jnp.float32
+                    forward[...], twice, preferred_element_type=jnp.float32
                 ).astype(jnp.bfloat16)
         if s == 0:
             coulomb_copy.wait()
@@ -201,6 +220,9 @@
 
     def slab_part():
         slab_copy.wait()
+        for s in range(share):
+            row = rows[pl.ds(peers * band + inner + s, 1), :NOCC]
+            own_scaled[s * TIMES : (s + 1) * TIMES] = (row * decay[:, :NOCC]).astype(jnp.bfloat16)
         green[...] = jnp.dot(own_scaled[...], slab[...], preferred_element_type=jnp.float32)
 
     def finish(s):
@@ -211,7 +233,7 @@
             total = total + sum_recv[s, h - 1].astype(jnp.float32)
         resummed = total / jnp.sqrt(1.0 + total * total)
         by_time = jnp.dot(
-            backward_ref[...], resummed, preferred_element_type=jnp.float32,
+            backward[...], resummed, preferred_element_type=jnp.float32,
             precision=lax.Precision.HIGHEST,
         )
         result = by_time * green[s * TIMES : (s + 1) * TIMES]
@@ -222,18 +244,17 @@
             out_copy(s, d).start()
         own_copy(s).start()
 
-    for s in range(share):
-        between = {}
-        if s > 0:
-            between[0] = functools.partial(pair_up, s - 1)
-        if s > 1:
-            between[1] = functools.partial(finish, s - 2)
-        green_loop(s, between)
-        if s == 0:
+    first_green()
+    screen(0)
+    for s in range(1, share):
+        green_loop(s)
+        if s == 1:
             slab_part()
+        if 1 < s < share - 1:
+            finish(s - 2)
         screen(s)
     pair_up(share - 1)
-    for s in range(max(share - 2, 0), share):
+    for s in range(max(share - 3, 0), share):
         finish(s)
     for s in range(share):
         half_copy(s).wait_send()
@@ -254,17 +275,16 @@
     slab = psi_slab.shape[1]
     chunk = owners * TIMES
     halves = chunk // CORES
-    _, backward = transform_tables()
+    _, to_times = transform_tables()
     bf16, f32 = jnp.bfloat16, jnp.float32
-    anywhere = pl.BlockSpec(memory_space=pl.ANY)
-    inside = pl.BlockSpec(memory_space=pltpu.VMEM)
+    outside = pl.BlockSpec(memory_space=pltpu.HBM)
     dma = pltpu.SemaphoreType.DMA
     return pl.pallas_call(
         functools.partial(kernel, sizes),
         name="gw_window",
         out_shape=jax.ShapeDtypeStruct((teams * share, TIMES // teams, slab), f32),
-        in_specs=[anywhere, anywhere, anywhere, inside, inside, anywhere, inside, inside],
-        out_specs=anywhere,
+        in_specs=[outside] * 8,
+        out_specs=pl.BlockSpec(memory_space=pl.ANY),
         scratch_shapes=[
             pltpu.VMEM((owners * band, orbitals), bf16),
             pltpu.VMEM((owners * band, orbitals), f32),
@@ -285,9 +305,12 @@
             pltpu.VMEM((share, TIMES, slab), f32),
             pltpu.VMEM((share * TIMES, slab), f32),
             pltpu.VMEM((share, teams, TIMES // teams, slab), f32),
+            pltpu.VMEM((1, orbitals), f32),
+            pltpu.VMEM((halves, CORES * halves), bf16),
+            pltpu.VMEM((TIMES, TIMES), f32),
             dma((owners,)),
             dma((points // TILE,)),
-            dma((2,)),
+            dma((6,)),
             dma((share,)),
             dma((share,)),
             dma((share, peers - 1)),
@@ -297,11 +320,11 @@
             dma((share,)),
         ],
         compiler_params=pltpu.CompilerParams(
-            collective_id=0, has_side_effects=True, vmem_limit_bytes=60 * 1024 * 1024
+            collective_id=0, has_side_effects=True, vmem_limit_bytes=53 * 1024 * 1024
         ),
     )(
         psi_rows, psi_cols, psi_slab, occ_depth[None], virt_height[None], coulomb,
-        jnp.asarray(forward_blocks(peers)), jnp.asarray(backward),
+        jnp.asarray(forward_blocks(peers)), jnp.asarray(to_times),
     )
 
 

time: 48.6 us -> 45.1 us (0.928)
  Pallas kernels: 46.8 us -> 41.1 us
  local copies, waits for them, and re-layouts: 1.67 us -> 3.65 us
    pallas_call x1, Pallas kernels: 46.8 us -> 41.1 us  [per_device(): pl.pallas_call(functools.partial(kernel, sizes), name='gw_window', out_sh...]
    unnamed x1 -> x9, local copies, waits for them, and re-layouts: 1.67 us -> 3.65 us
where the time goes in v4:
time: 45.1 us; the launch traced here: 44.8 us
  Pallas kernels  41.1 us (91%)
  local copies, waits for them, and re-layouts  3.65 us (8%)
    pallas_call x1, Pallas kernels, per_device(): pl.pallas_call(functools.partial(kernel, sizes), name='gw_window', out_sh...  41.1 us
    unnamed x9, local copies, waits for them, and re-layouts  3.65 us

profile of v4, /device:TPU:0, one launch (start us, length us, event | category | flops | bytes accessed | tf_op | source)
XLA Modules:
  0.0 44.8 jit_solution(6362490549885146221)
XLA Ops:
  0.0 0.0 copy-start
  0.0 0.8 %copy-done = bf16[128,256]{1,0:T(8,128)(2,1)S(1)} copy-done((bf16[128,256]{1,0:T(8,128)(2,1)S(1)}, bf16[128,256]{1,0:T(8,128)(2,1)}, u32[]{:S(2)}) %copy-start) | copy-done | bytes 65560
  0.8 0.0 copy-start.1
  0.8 0.7 %copy-done.1 = f32[5120]{0:T(1024)S(1)} copy-done((f32[5120]{0:T(1024)S(1)}, f32[5120]{0:T(1024)}, u32[]{:S(2)}) %copy-start.1) | copy-done | bytes 20504
  1.6 0.0 copy-start.2
  1.6 0.7 %copy-done.2 = f32[16,16]{1,0:T(8,128)S(1)} copy-done((f32[16,16]{1,0:T(8,128)S(1)}, f32[16,16]{1,0:T(8,128)}, u32[]{:S(2)}) %copy-start.2) | copy-done | bytes 1048
  2.3 0.0 copy-start.3
  2.3 0.7 %copy-done.3 = f32[1024]{0:T(1024)S(1)} copy-done((f32[1024]{0:T(1024)S(1)}, f32[1024]{0:T(1024)}, u32[]{:S(2)}) %copy-start.3) | copy-done | bytes 4120
  3.0 41.1 %gw_window.1 = f32[32,2,1024]{2,1,0:T(2,128)S(1)} custom-call(bf16[512,6144]{1,0:T(8,128)(2,1)} %rows_hbm.1, bf16[6144,1024]{1,0:T(8,128)(2,1)} %cols_hbm.1, bf16[1024,1024]{1,0:T(8,128)(2,1)} %slab_hbm.1, f32[1,1024]{1,0:T(1,128)S(1)} %bitcast.3, f32[1,5120]{1,0:T(1,128)S(1)} %bitcast.2, bf16[1024,1024]{1,0:T(8,128)(2,1)} %coulomb_hbm.1, ...), custom_call_target="tpu_custom_call" | custom-call | tf_op jit(solution)/shard_map/gw_window/pallas_call | solution.py:282
  44.0 0.7 %copy.10 = f32[32,2,1024]{2,1,0:T(2,128)} copy(f32[32,2,1024]{2,1,0:T(2,128)S(1)} %gw_window.1) | data formatting | bytes 524288
Async XLA Ops:
  0.0 0.8 %copy-start = (bf16[128,256]{1,0:T(8,128)(2,1)S(1)}, bf16[128,256]{1,0:T(8,128)(2,1)}, u32[]{:S(2)}) copy-start(bf16[128,256]{1,0:T(8,128)(2,1)} %constant.4.clone.forward_hbm) | copy-start | bytes 196612
  0.8 0.7 %copy-start.1 = (f32[5120]{0:T(1024)S(1)}, f32[5120]{0:T(1024)}, u32[]{:S(2)}) copy-start(f32[5120]{0:T(1024)} %param.12) | copy-start | bytes 61444
  1.6 0.7 %copy-start.2 = (f32[16,16]{1,0:T(8,128)S(1)}, f32[16,16]{1,0:T(8,128)}, u32[]{:S(2)}) copy-start(f32[16,16]{1,0:T(8,128)} %constant.5.clone.backward_hbm) | copy-start | bytes 3076
  2.3 0.7 %copy-start.3 = (f32[1024]{0:T(1024)S(1)}, f32[1024]{0:T(1024)}, u32[]{:S(2)}) copy-start(f32[1024]{0:T(1024)} %param.11) | copy-start | bytes 12292
